TPU v7x, 32 devices: a whole 2x2x4 slice. The times are simulated.
32 devices in a mesh: dp: 4 (over z), mp: 8 (over y, x, core).
Axes of the slice: x: 2, y: 2, z: 4, core: 2. Of those that a mesh axis runs over, the one named last changes fastest.
Arguments:
- block_input: bfloat16 [8192, 2048], P(('dp', 'mp')), may hold values from -6 to 6
- out_cotangent: bfloat16 [8192, 2048], P(('dp', 'mp')), may hold values from -6 to 6
- objective: int32 [16], P('dp'), may hold values from 0 to 1, as said below
- prefix_len: int32 [16], P('dp'), may hold values from 64 to 511
- target_mask: int32 [8192], P(('dp', 'mp')), may hold values from 0 to 1, as said below
- qkv_weight: float32 [2048, 3, 2048], P('dp', None, 'mp'), may hold values from -0.125 to 0.125
- out_weight: float32 [2048, 2048], P('mp', 'dp'), may hold values from -3 to 3
- gateup_weight: float32 [2048, 2, 5472], P('dp', None, 'mp'), may hold values from -0.125 to 0.125
- down_weight: float32 [5472, 2048], P('mp', 'dp'), may hold values from -0.625 to 0.625
- norm_params: float32 [4, 2048], replicated, as said below
- qkv_first: float32 [2048, 3, 2048], P('dp', None, 'mp'), may hold values from -0.125 to 0.125
- out_first: float32 [2048, 2048], P('mp', 'dp'), may hold values from -0.005859375 to 0.005859375
- gateup_first: float32 [2048, 2, 5472], P('dp', None, 'mp'), may hold values from -0.09375 to 0.09375
- down_first: float32 [5472, 2048], P('mp', 'dp'), may hold values from -0.013671875 to 0.013671875
- norm_first: float32 [4, 2048], replicated, may hold values from -0.21875 to 0.21875
- qkv_second: float32 [2048, 3, 2048], P('dp', None, 'mp'), may hold values from 3.0517578e-05 to 0.00048828125
- out_second: float32 [2048, 2048], P('mp', 'dp'), may hold values from 7.080078e-08 to 1.1230469e-06
- gateup_second: float32 [2048, 2, 5472], P('dp', None, 'mp'), may hold values from 1.953125e-05 to 0.0003125
- down_second: float32 [5472, 2048], P('mp', 'dp'), may hold values from 4.3945312e-07 to 7.080078e-06
- norm_second: float32 [4, 2048], replicated, may hold values from 0.00012207031 to 0.001953125
Outputs:
- block_output: bfloat16 [8192, 2048], P(('dp', 'mp'))
- input_grad: float32 [8192, 2048], P(('dp', 'mp'))
- qkv_new: float32 [2048, 3, 2048], P('dp', None, 'mp')
- qkv_first_new: float32 [2048, 3, 2048], P('dp', None, 'mp')
- qkv_second_new: float32 [2048, 3, 2048], P('dp', None, 'mp')
- out_new: float32 [2048, 2048], P('mp', 'dp')
- out_first_new: float32 [2048, 2048], P('mp', 'dp')
- out_second_new: float32 [2048, 2048], P('mp', 'dp')
- gateup_new: float32 [2048, 2, 5472], P('dp', None, 'mp')
- gateup_first_new: float32 [2048, 2, 5472], P('dp', None, 'mp')
- gateup_second_new: float32 [2048, 2, 5472], P('dp', None, 'mp')
- down_new: float32 [5472, 2048], P('mp', 'dp')
- down_first_new: float32 [5472, 2048], P('mp', 'dp')
- down_second_new: float32 [5472, 2048], P('mp', 'dp')
- norm_new: float32 [4, 2048], replicated
- norm_first_new: float32 [4, 2048], replicated
- norm_second_new: float32 [4, 2048], replicated
Inputs may be any that keep to these rules, and one draw needn't show every extreme that they name: `objective`: at least one sequence of each kind. `target_mask`: the last residue of every sequence is a target. `norm_params`: rows 0 and 2 are the gains of the first and second norm, rows 1 and 3 their biases.
All inputs are finite; a program needn't handle non-finite values.
Results may differ from a plain program's by a relative error of at most 0.024.
Values may be sent and summed in bfloat16 or wider, within the bound.
No kernel may reach another device: no remote copies, remote signals or barrier semaphores. Data moves between devices by JAX's collectives and lax.ppermute only.
A program may use at most 256 MiB of HBM per device.

v0:
```python
import jax
import jax.numpy as jnp
from jax import lax
from jax.sharding import PartitionSpec as P

D = 2048
HD = 128
FF = 5461
FF_PAD = 5472
STEP = 5
deep_alpha = 48.0**0.5
norm_eps = 1e-05
masked_score = -1e30
rope_base = 10000.0
beta_one = 0.5
beta_two = 0.5
adam_eps = 1e-08
decay_rate = 0.1


def rope_tables(seq_len, head_dim):
    position = jnp.arange(seq_len, dtype=jnp.float32)
    freqs = rope_base ** (-jnp.arange(0, head_dim, 2, dtype=jnp.float32) / head_dim)
    angles = position[:, None] * freqs[None, :]
    return (jnp.cos(angles), jnp.sin(angles))


def rotate(values, cosine, sine_table):
    half_dim = values.shape[-1] // 2
    first_half = values[..., :half_dim]
    second_half = values[..., half_dim:]
    cos_b = cosine[:, None, :]
    sin_b = sine_table[:, None, :]
    return jnp.concatenate(
        [first_half * cos_b - second_half * sin_b, second_half * cos_b + first_half * sin_b], -1
    )


def norm_forward(hidden, norm_gain, norm_bias):
    row_mean = jnp.mean(hidden, -1, keepdims=True)
    centred = hidden - row_mean
    variance = jnp.mean(centred * centred, -1, keepdims=True)
    inv_std = lax.rsqrt(variance + norm_eps)
    normed = centred * inv_std
    return (normed * norm_gain + norm_bias, normed, inv_std)


def norm_backward(grad_rows, normed, inv_std, norm_gain):
    grad_normed = grad_rows * norm_gain
    mean_grad = jnp.mean(grad_normed, -1, keepdims=True)
    mean_proj = jnp.mean(grad_normed * normed, -1, keepdims=True)
    grad_in = inv_std * (grad_normed - mean_grad - normed * mean_proj)
    return (grad_in, jnp.sum(grad_rows * normed, 0), jnp.sum(grad_rows, 0))


def adamw(weight, gradient, first_moment, second, step_rate):
    first_new = beta_one * first_moment + (1.0 - beta_one) * gradient
    second_new = beta_two * second + (1.0 - beta_two) * gradient * gradient
    first_hat = first_new / (1.0 - beta_one**STEP)
    second_hat = second_new / (1.0 - beta_two**STEP)
    weight_new = weight - step_rate * (
        first_hat / (jnp.sqrt(second_hat) + adam_eps) + decay_rate * weight
    )
    return (weight_new, first_new, second_new)


def local(
    block_input,
    out_cotangent,
    objective,
    prefix_len,
    target_mask,
    qkv_weight,
    out_weight,
    gateup_weight,
    down_weight,
    norm_params,
    qkv_first,
    out_first,
    gateup_first,
    down_first,
    norm_first,
    qkv_second,
    out_second,
    gateup_second,
    down_second,
    norm_second,
):
    mp_count = lax.axis_size("mp")
    mp_index = lax.axis_index("mp")
    own_rows = block_input.shape[0]
    seq_count = objective.shape[0]
    group_rows = own_rows * mp_count
    seq_len = group_rows // seq_count
    local_dim = qkv_weight.shape[2]
    local_heads = local_dim // HD
    local_units = gateup_weight.shape[2]
    score_scale = HD ** (-0.5)
    row_start = mp_index * own_rows
    qkv_full, out_full, gateup_full, down_full = (
        lax.all_gather(qkv_weight.astype(jnp.bfloat16), "dp", axis=0, tiled=True),
        lax.all_gather(out_weight.astype(jnp.bfloat16), "dp", axis=1, tiled=True),
        lax.all_gather(gateup_weight.astype(jnp.bfloat16), "dp", axis=0, tiled=True),
        lax.all_gather(down_weight.astype(jnp.bfloat16), "dp", axis=1, tiled=True),
    )
    input_all = lax.all_gather(block_input, "mp", axis=0, tiled=True)
    projected = jnp.einsum("td,dce->tce", input_all, qkv_full, preferred_element_type=jnp.float32)
    shaped = projected.reshape(seq_count, seq_len, 3, local_heads, HD)
    cosine, sine_table = rope_tables(seq_len, HD)
    query_rows = rotate(shaped[:, :, 0], cosine, sine_table).astype(jnp.bfloat16)
    key_rows = rotate(shaped[:, :, 1], cosine, sine_table).astype(jnp.bfloat16)
    value_rows = shaped[:, :, 2].astype(jnp.bfloat16)
    row_index = jnp.arange(seq_len)[:, None]
    col_index = jnp.arange(seq_len)[None, :]
    visible = (
        (objective[:, None, None] > 0)
        | (col_index[None] < prefix_len[:, None, None])
        | (col_index <= row_index)[None]
    )
    scores = (
        jnp.einsum("sihe,sjhe->shij", query_rows, key_rows, preferred_element_type=jnp.float32)
        * score_scale
    )
    scores = jnp.where(visible[:, None], scores, masked_score)
    row_max = jnp.max(scores, -1, keepdims=True)
    exp_scores = jnp.exp(scores - row_max)
    row_total = jnp.sum(exp_scores, -1, keepdims=True)
    soft_weights = exp_scores / row_total
    log_total = row_max + jnp.log(row_total)
    attended = jnp.einsum(
        "shij,sjhe->sihe",
        soft_weights.astype(jnp.bfloat16),
        value_rows,
        preferred_element_type=jnp.float32,
    )
    attended_low = attended.reshape(group_rows, local_dim).astype(jnp.bfloat16)
    attn_part = jnp.dot(attended_low, out_full, preferred_element_type=jnp.float32)
    attn_total = lax.psum(attn_part, "mp")
    hidden_all = deep_alpha * input_all.astype(jnp.float32) + attn_total
    middle_all, _, _ = norm_forward(hidden_all, norm_params[0], norm_params[1])
    middle_low = middle_all.astype(jnp.bfloat16)
    hidden_one = lax.dynamic_slice_in_dim(hidden_all, row_start, own_rows, 0)
    middle = lax.dynamic_slice_in_dim(middle_all, row_start, own_rows, 0)
    live_units = (mp_index * local_units + jnp.arange(local_units) < FF).astype(jnp.float32)
    gate_up = jnp.einsum("td,dcf->tcf", middle_low, gateup_full, preferred_element_type=jnp.float32)
    hidden_low = (jax.nn.gelu(gate_up[:, 0]) * gate_up[:, 1] * live_units).astype(jnp.bfloat16)
    ffn_part = jnp.dot(hidden_low, down_full, preferred_element_type=jnp.float32)
    ffn_total = lax.psum(ffn_part.astype(jnp.bfloat16), "mp").astype(jnp.float32)
    ffn_own = lax.dynamic_slice_in_dim(ffn_total, row_start, own_rows, 0)
    hidden_two = deep_alpha * middle + ffn_own
    output_rows, normed_two, inv_two = norm_forward(hidden_two, norm_params[2], norm_params[3])
    mask_f32 = target_mask.astype(jnp.float32)
    grad_rows = out_cotangent.astype(jnp.float32) * mask_f32[:, None]
    grad_two, gain_two, bias_two = norm_backward(grad_rows, normed_two, inv_two, norm_params[2])
    ffn_back = lax.all_gather(grad_two.astype(jnp.bfloat16), "mp", axis=0, tiled=True)
    gate_again = jnp.einsum(
        "td,dcf->tcf", middle_low, gateup_full, preferred_element_type=jnp.float32
    )
    gate_act, gelu_pull = jax.vjp(jax.nn.gelu, gate_again[:, 0])
    up_part = gate_again[:, 1]
    hidden_again = (gate_act * up_part * live_units).astype(jnp.bfloat16)
    grad_hidden = (
        jnp.einsum("td,fd->tf", ffn_back, down_full, preferred_element_type=jnp.float32)
        * live_units
    )
    down_grad = jnp.einsum("tf,td->fd", hidden_again, ffn_back, preferred_element_type=jnp.float32)
    grad_gate = gelu_pull(grad_hidden * up_part)[0]
    grad_up = grad_hidden * gate_act
    grad_gateup = jnp.stack([grad_gate, grad_up], 1).astype(jnp.bfloat16)
    middle_part = jnp.einsum(
        "tcf,dcf->td", grad_gateup, gateup_full, preferred_element_type=jnp.float32
    )
    gateup_grad = jnp.einsum(
        "td,tcf->dcf", middle_low, grad_gateup, preferred_element_type=jnp.float32
    )
    grad_middle = (
        lax.psum_scatter(
            middle_part.astype(jnp.bfloat16), "mp", scatter_dimension=0, tiled=True
        ).astype(jnp.float32)
        + deep_alpha * grad_two
    )
    _, normed_one, inv_one = norm_forward(hidden_one, norm_params[0], norm_params[1])
    grad_one, gain_one, bias_one = norm_backward(grad_middle, normed_one, inv_one, norm_params[0])
    attn_back = lax.all_gather(grad_one.astype(jnp.bfloat16), "mp", axis=0, tiled=True)
    grad_attended = jnp.einsum(
        "td,ed->te", attn_back, out_full, preferred_element_type=jnp.float32
    ).astype(jnp.bfloat16)
    grad_attended = grad_attended.reshape(seq_count, seq_len, local_heads, HD)
    out_grad = jnp.einsum("te,td->ed", attended_low, attn_back, preferred_element_type=jnp.float32)
    scores_again = (
        jnp.einsum("sihe,sjhe->shij", query_rows, key_rows, preferred_element_type=jnp.float32)
        * score_scale
    )
    scores_again = jnp.where(visible[:, None], scores_again, masked_score)
    soft_again = jnp.exp(scores_again - log_total)
    grad_soft = jnp.einsum(
        "sihe,sjhe->shij", grad_attended, value_rows, preferred_element_type=jnp.float32
    )
    value_grad = jnp.einsum(
        "shij,sihe->sjhe",
        soft_again.astype(jnp.bfloat16),
        grad_attended,
        preferred_element_type=jnp.float32,
    )
    row_dot = jnp.sum(soft_again * grad_soft, -1, keepdims=True)
    grad_scores = (soft_again * (grad_soft - row_dot)).astype(jnp.bfloat16)
    query_grad = (
        jnp.einsum("shij,sjhe->sihe", grad_scores, key_rows, preferred_element_type=jnp.float32)
        * score_scale
    )
    key_grad = (
        jnp.einsum("shij,sihe->sjhe", grad_scores, query_rows, preferred_element_type=jnp.float32)
        * score_scale
    )
    query_lin = rotate(query_grad, cosine, -sine_table)
    key_lin = rotate(key_grad, cosine, -sine_table)
    grad_proj = (
        jnp.stack([query_lin, key_lin, value_grad], 2)
        .astype(jnp.bfloat16)
        .reshape(group_rows, 3, local_dim)
    )
    input_part = jnp.einsum("tce,dce->td", grad_proj, qkv_full, preferred_element_type=jnp.float32)
    qkv_grad = jnp.einsum("td,tce->dce", input_all, grad_proj, preferred_element_type=jnp.float32)
    input_raw = (
        lax.psum_scatter(
            input_part.astype(jnp.bfloat16), "mp", scatter_dimension=0, tiled=True
        ).astype(jnp.float32)
        + deep_alpha * grad_one
    )
    qkv_grad, out_grad, gateup_grad, down_grad = (
        lax.psum_scatter(
            qkv_grad.astype(jnp.bfloat16), "dp", scatter_dimension=0, tiled=True
        ).astype(jnp.float32),
        lax.psum_scatter(
            out_grad.astype(jnp.bfloat16), "dp", scatter_dimension=1, tiled=True
        ).astype(jnp.float32),
        lax.psum_scatter(
            gateup_grad.astype(jnp.bfloat16), "dp", scatter_dimension=0, tiled=True
        ).astype(jnp.float32),
        lax.psum_scatter(
            down_grad.astype(jnp.bfloat16), "dp", scatter_dimension=1, tiled=True
        ).astype(jnp.float32),
    )
    norm_grad = jnp.stack([gain_one, bias_one, gain_two, bias_two], 0)
    norm_grad, target_count = lax.psum((norm_grad, jnp.sum(mask_f32)), ("dp", "mp"))
    rate_list = (D ** (-0.5), 0.5, D ** (-0.5), (FF_PAD // 64) ** (-0.5), 0.4)
    qkv_res = adamw(qkv_weight, qkv_grad / target_count, qkv_first, qkv_second, rate_list[0])
    out_res = adamw(out_weight, out_grad / target_count, out_first, out_second, rate_list[1])
    gateup_res = adamw(
        gateup_weight, gateup_grad / target_count, gateup_first, gateup_second, rate_list[2]
    )
    down_res = adamw(down_weight, down_grad / target_count, down_first, down_second, rate_list[3])
    norm_res = adamw(norm_params, norm_grad / target_count, norm_first, norm_second, rate_list[4])
    return (
        output_rows.astype(jnp.bfloat16),
        input_raw / target_count,
        qkv_res[0],
        qkv_res[1],
        qkv_res[2],
        out_res[0],
        out_res[1],
        out_res[2],
        gateup_res[0],
        gateup_res[1],
        gateup_res[2],
        down_res[0],
        down_res[1],
        down_res[2],
        norm_res[0],
        norm_res[1],
        norm_res[2],
    )


def solution(mesh):
    return jax.shard_map(
        local,
        mesh=mesh,
        in_specs=(
            P(("dp", "mp"), None),
            P(("dp", "mp"), None),
            P("dp"),
            P("dp"),
            P(("dp", "mp")),
            P("dp", None, "mp"),
            P("mp", "dp"),
            P("dp", None, "mp"),
            P("mp", "dp"),
            P(),
            P("dp", None, "mp"),
            P("mp", "dp"),
            P("dp", None, "mp"),
            P("mp", "dp"),
            P(),
            P("dp", None, "mp"),
            P("mp", "dp"),
            P("dp", None, "mp"),
            P("mp", "dp"),
            P(),
        ),
        out_specs=(
            P(("dp", "mp"), None),
            P(("dp", "mp"), None),
            P("dp", None, "mp"),
            P("dp", None, "mp"),
            P("dp", None, "mp"),
            P("mp", "dp"),
            P("mp", "dp"),
            P("mp", "dp"),
            P("dp", None, "mp"),
            P("dp", None, "mp"),
            P("dp", None, "mp"),
            P("mp", "dp"),
            P("mp", "dp"),
            P("mp", "dp"),
            P(),
            P(),
            P(),
        ),
        check_vma=False,
    )
```

profile of v0, /device:TPU:0, one launch (start us, length us, event | category | flops | bytes accessed | tf_op | source)
XLA Modules:
  0.0 1279.1 jit_solution(2433256142239264889)
XLA Ops:
  14.7 61.7 %all-gather.10.cloned.1.call-done = bf16[2048,3,256]{2,0,1:T(8,128)(2,1)} async-done(((bf16[512,3,256]{2,0,1:T(8,128)(2,1)}), bf16[2048,3,256]{2,0,1:T(8,128)(2,1)}) %all-gather.10.cloned.1.call-update) | async-done | bytes 3145744 | tf_op jit(solution)/shard_map/all_gather | solution.py:101
  76.4 54.8 %all-gather.8.cloned.1.call-done = bf16[2048,2048]{1,0:T(8,128)(2,1)} async-done(((bf16[256,2048]{1,0:T(8,128)(2,1)}), bf16[2048,2048]{1,0:T(8,128)(2,1)}) %all-gather.8.cloned.1.call-update) | async-done | bytes 8388624 | tf_op jit(solution)/shard_map/all_gather | solution.py:106
  131.2 11.6 fusion.6
  173.4 11.4 copy.105
  200.8 211.6 %all-reduce.4.cloned.1.call-done = f32[2048,2048]{1,0:T(8,128)} async-done(((f32[2048,2048]{1,0:T(8,128)}), f32[2048,2048]{1,0:T(8,128)}) %all-reduce.4.cloned.1.call-update) | async-done | bytes 16777232 | tf_op jit(solution)/shard_map/psum | solution.py:138
  412.5 16.0 %fusion.81 = (f32[2048]{0:T(1024)S(1)}, f32[2048,2048]{1,0:T(8,128)}) fusion(f32[2048,2048]{1,0:T(8,128)} %all-reduce.4.cloned.1.call-done, bf16[2048,2048]{1,0:T(8,128)(2,1)} %all-gather.8.cloned.1.call-done), kind=kLoop, calls=%fused_computation.166 | loop fusion | flops 16775168 | bytes 41951232 | tf_op jit(solution)/shard_map/reduce_sum | solution.py:40
  436.2 12.2 multiply_add_fusion
  448.5 69.6 %all-gather.14.cloned.1.call-done = bf16[2048,2,684]{0,1,2:T(2,128)(2,1)} async-done(((bf16[512,2,684]{0,1,2:T(2,128)(2,1)}), bf16[2048,2,684]{0,1,2:T(2,128)(2,1)}) %all-gather.14.cloned.1.call-update) | async-done | bytes 5603344 | tf_op jit(solution)/shard_map/all_gather | solution.py:103
  518.1 22.3 %fusion.2 = f32[2048,2,684]{0,2,1:T(8,128)} fusion(bf16[2048,2,684]{0,1,2:T(2,128)(2,1)} %all-gather.14.cloned.1.call-done, f32[2048,2048]{1,0:T(8,128)} %multiply_add_fusion), kind=kOutput, calls=%fused_computation.7 | convolution fusion | flops 11479810048 | bytes 33587200 | tf_op jit(solution)/shard_map/td,dcf->tcf/dot_general | solution.py:145
  545.8 30.5 %all-gather.16.cloned.1.call-done = bf16[684,2048]{1,0:T(8,128)(2,1)} async-done(((bf16[684,512]{1,0:T(8,128)(2,1)}), bf16[684,2048]{1,0:T(8,128)(2,1)}) %all-gather.16.cloned.1.call-update) | async-done | bytes 2801680 | tf_op jit(solution)/shard_map/all_gather | solution.py:104
  576.3 11.2 convolution_convert_fusion
  588.2 124.4 %all-reduce.6.cloned.1.call-done = bf16[2048,2048]{1,0:T(8,128)(2,1)} async-done(((bf16[2048,2048]{1,0:T(8,128)(2,1)}), bf16[2048,2048]{1,0:T(8,128)(2,1)}) %all-reduce.6.cloned.1.call-update) | async-done | bytes 8388624 | tf_op jit(solution)/shard_map/psum | solution.py:148
  719.2 54.5 %all-gather.18.cloned.1.call-done = bf16[2048,2048]{1,0:T(8,128)(2,1)} async-done(((bf16[256,2048]{1,0:T(8,128)(2,1)}), bf16[2048,2048]{1,0:T(8,128)(2,1)}) %all-gather.18.cloned.1.call-update) | async-done | bytes 8388624 | tf_op jit(solution)/shard_map/all_gather | solution.py:155
  773.7 15.4 %fusion.36 = (bf16[2048,1,684]{0,2,1:T(8,128)(2,1)S(1)}, bf16[2048,1,684]{0,2,1:T(8,128)(2,1)S(1)}) fusion(f32[2048,2,684]{0,2,1:T(8,128)} %fusion.2, f32[684]{0:T(1024)S(1)} %fusion.66, bf16[2048,2048]{1,0:T(8,128)(2,1)} %all-gather.18.cloned.1.call-done, bf16[684,2048]{1,0:T(8,128)(2,1)} %all-gather.16.cloned.1.call-done), kind=kOutput, calls=%fused_computation.56 | convolution fusion | flops 5772828672 | bytes 28002992 | tf_op jit(solution)/shard_map/td,fd->tf/dot_general | solution.py:163
  791.6 17.9 %bitcast_convert_fusion.1 = bf16[2048,2048]{1,0:T(8,128)(2,1)} fusion(bf16[2048,2,684]{0,1,2:T(2,128)(2,1)} %all-gather.14.cloned.1.call-done, bf16[2048,1,684]{0,2,1:T(8,128)(2,1)S(1)} %get-tuple-element.102, bf16[2048,1,684]{0,2,1:T(8,128)(2,1)S(1)} %get-tuple-element.101), kind=kOutput, calls=%fused_computation.1 | convolution fusion | flops 11482611712 | bytes 19595264 | tf_op jit(solution)/shard_map/tcf,dcf->td/dot_general | solution.py:170
  813.5 67.7 %reduce-scatter.7.cloned.1.call-done = bf16[256,2048]{1,0:T(8,128)(2,1)} async-done(((bf16[2048,2048]{1,0:T(8,128)(2,1)}), bf16[256,2048]{1,0:T(8,128)(2,1)}) %reduce-scatter.7.cloned.1.call-update) | async-done | bytes 1048592 | tf_op jit(solution)/shard_map/reduce_scatter | solution.py:177
  888.4 18.6 %fusion.19 = bf16[2048,2,684]{0,2,1:T(8,128)(2,1)} fusion(f32[2048,2048]{1,0:T(8,128)} %multiply_add_fusion, bf16[2048,1,684]{0,2,1:T(8,128)(2,1)} %copy-done.49, bf16[2048,1,684]{0,2,1:T(8,128)(2,1)} %copy-done.48), kind=kOutput, calls=%fused_computation.39 | convolution fusion | flops 11493818368 | bytes 27983872 | tf_op jit(solution)/shard_map/td,tcf->dcf/dot_general | solution.py:173
  920.2 22.6 %all-gather.20.cloned.1.call-done = bf16[2048,2048]{1,0:T(8,128)(2,1)} async-done(((bf16[256,2048]{1,0:T(8,128)(2,1)}), bf16[2048,2048]{1,0:T(8,128)(2,1)}) %all-gather.20.cloned.1.call-update) | async-done | bytes 8388624 | tf_op jit(solution)/shard_map/all_gather | solution.py:184
  993.3 12.0 fusion.31
  1027.8 41.6 %all-reduce = (f32[]{:T(128)}, f32[4,2048]{1,0:T(4,128)S(1)}) all-reduce(f32[]{:T(128)} %convert_reduce_fusion, f32[4,2048]{1,0:T(4,128)S(1)} %pad_maximum_fusion.11), channel_id=1, replica_groups=mesh['dp'=4,'mp'=8] {'dp','mp'}, use_global_device_ids=true, to_apply=%region_18.19 | all-reduce | flops 8193 | bytes 65544 | tf_op jit(solution)/shard_map/psum | solution.py:245
  1087.2 16.2 %reduce-scatter.17.cloned.1.call-done = bf16[684,512]{1,0:T(8,128)(2,1)} async-done(((bf16[684,2048]{1,0:T(8,128)(2,1)}), bf16[684,512]{1,0:T(8,128)(2,1)}) %reduce-scatter.17.cloned.1.call-update) | async-done | bytes 700432 | tf_op jit(solution)/shard_map/reduce_scatter | solution.py:240
  1108.6 24.2 %reduce-scatter.13.cloned.1.call-done = bf16[256,512]{1,0:T(8,128)(2,1)} async-done(((bf16[256,2048]{1,0:T(8,128)(2,1)}), bf16[256,512]{1,0:T(8,128)(2,1)}) %reduce-scatter.13.cloned.1.call-update) | async-done | bytes 262160 | tf_op jit(solution)/shard_map/reduce_scatter | solution.py:234
  1136.4 57.5 %reduce-scatter.11.cloned.1.call-done = bf16[512,3,256]{0,2,1:T(8,128)(2,1)} async-done(((bf16[2048,3,256]{0,2,1:T(8,128)(2,1)}), bf16[512,3,256]{0,2,1:T(8,128)(2,1)}) %reduce-scatter.11.cloned.1.call-update) | async-done | bytes 786448 | tf_op jit(solution)/shard_map/reduce_scatter | solution.py:231
  1208.9 59.7 %reduce-scatter.9.cloned.1.call-done = bf16[256,2048]{1,0:T(8,128)(2,1)} async-done(((bf16[2048,2048]{1,0:T(8,128)(2,1)}), bf16[256,2048]{1,0:T(8,128)(2,1)}) %reduce-scatter.9.cloned.1.call-update) | async-done | bytes 1048592 | tf_op jit(solution)/shard_map/reduce_scatter | solution.py:225
  (216 shorter events, 219.0 us)
Async XLA Ops:
  7.2 69.1 %all-gather.10.cloned.1.call-start = ((), (), s32[]{:S(2)}) async-start(), calls=%async_computation.7 | async-start | bytes 3932160 | tf_op jit(solution)/shard_map/all_gather | solution.py:101
  9.7 121.5 %all-gather.8.cloned.1.call-start = ((), (), s32[]{:S(2)}) async-start(), calls=%async_computation.6 | async-start | bytes 9437184 | tf_op jit(solution)/shard_map/all_gather | solution.py:106
  10.5 174.4 %all-gather.12.cloned.1.call-start = ((), (), s32[]{:S(2)}) async-start(), calls=%async_computation.8 | async-start | bytes 1310720 | tf_op jit(solution)/shard_map/all_gather | solution.py:102
  11.3 401.2 %all-reduce.4.cloned.1.call-start = ((), (), s32[]{:S(2)}) async-start(), calls=%async_computation.9 | async-start | bytes 33554432 | tf_op jit(solution)/shard_map/psum | solution.py:138
  13.2 150.0 %copy-start.26 = (f32[512,64]{1,0:T(8,128)}, f32[512,64]{1,0:T(8,128)S(1)}, u32[]{:S(2)}) copy-start(f32[512,64]{1,0:T(8,128)S(1)} %get-tuple-element.124) | copy-start | bytes 393220
  194.5 323.5 %all-gather.14.cloned.1.call-start = ((), (), s32[]{:S(2)}) async-start(), calls=%async_computation.10 | async-start | bytes 7004160 | tf_op jit(solution)/shard_map/all_gather | solution.py:103
  198.4 377.9 %all-gather.16.cloned.1.call-start = ((), (), s32[]{:S(2)}) async-start(), calls=%async_computation.11 | async-start | bytes 3522560 | tf_op jit(solution)/shard_map/all_gather | solution.py:104
  200.7 511.8 %all-reduce.6.cloned.1.call-start = ((), (), s32[]{:S(2)}) async-start(), calls=%async_computation.12 | async-start | bytes 16777216 | tf_op jit(solution)/shard_map/psum | solution.py:148
  545.8 41.6 %copy-start.24 = (bf16[2048,684]{0,1:T(8,128)(2,1)}, bf16[2048,684]{0,1:T(8,128)(2,1)S(1)}, u32[]{:S(2)}) copy-start(bf16[2048,684]{0,1:T(8,128)(2,1)S(1)} %multiply_convert_fusion.2) | copy-start | bytes 8404996
  587.5 186.2 %all-gather.18.cloned.1.call-start = ((), (), s32[]{:S(2)}) async-start(), calls=%async_computation.13 | async-start | bytes 9437184 | tf_op jit(solution)/shard_map/all_gather | solution.py:155
  588.2 127.0 %copy-start.20 = (bf16[256,2048]{1,0:T(8,128)(2,1)S(1)}, bf16[256,2048]{1,0:T(8,128)(2,1)}, u32[]{:S(2)}) copy-start(bf16[256,2048]{1,0:T(8,128)(2,1)} %param.21) | copy-start | bytes 3145732
  719.1 162.0 %reduce-scatter.7.cloned.1.call-start = ((), (), s32[]{:S(2)}) async-start(), calls=%async_computation.14 | async-start | bytes 9437184 | tf_op jit(solution)/shard_map/reduce_scatter | solution.py:177
  809.5 133.2 %all-gather.20.cloned.1.call-start = ((), (), s32[]{:S(2)}) async-start(), calls=%async_computation.15 | async-start | bytes 9437184 | tf_op jit(solution)/shard_map/all_gather | solution.py:184
  888.3 181.1 %reduce-scatter.15.cloned.1.call-start = ((), (), s32[]{:S(2)}) async-start(), calls=%async_computation.19 | async-start | bytes 7045120 | tf_op jit(solution)/shard_map/reduce_scatter | solution.py:237
  907.0 196.4 %reduce-scatter.17.cloned.1.call-start = ((), (), s32[]{:S(2)}) async-start(), calls=%async_computation.20 | async-start | bytes 3522560 | tf_op jit(solution)/shard_map/reduce_scatter | solution.py:240
  919.4 23.3 %copy-start.30 = (bf16[256,2048]{1,0:T(8,128)(2,1)S(1)}, bf16[256,2048]{1,0:T(8,128)(2,1)}, u32[]{:S(2)}) copy-start(bf16[256,2048]{1,0:T(8,128)(2,1)} %all-gather.12.cloned.1.call-done) | copy-start | bytes 3145732
  919.5 213.3 %reduce-scatter.13.cloned.1.call-start = ((), (), s32[]{:S(2)}) async-start(), calls=%async_computation.18 | async-start | bytes 1310720 | tf_op jit(solution)/shard_map/reduce_scatter | solution.py:234
  991.1 202.7 %reduce-scatter.11.cloned.1.call-start = ((), (), s32[]{:S(2)}) async-start(), calls=%async_computation.17 | async-start | bytes 3932160 | tf_op jit(solution)/shard_map/reduce_scatter | solution.py:231
  1005.3 263.3 %reduce-scatter.9.cloned.1.call-start = ((), (), s32[]{:S(2)}) async-start(), calls=%async_computation.16 | async-start | bytes 9437184 | tf_op jit(solution)/shard_map/reduce_scatter | solution.py:225
  1021.0 48.5 %copy-start.4 = (f32[512,2,684]{0,1,2:T(2,128)S(1)}, f32[512,2,684]{0,1,2:T(2,128)}, u32[]{:S(2)}) copy-start(f32[512,2,684]{0,1,2:T(2,128)} %param.27) | copy-start | bytes 8404996
  1082.1 21.3 %copy-start.19 = (f32[684,512]{1,0:T(8,128)S(1)}, f32[684,512]{1,0:T(8,128)}, u32[]{:S(2)}) copy-start(f32[684,512]{1,0:T(8,128)} %param.28) | copy-start | bytes 4202500
  1108.6 85.3 %copy-start.17 = (f32[512,3,256]{0,2,1:T(8,128)S(1)}, f32[512,3,256]{0,2,1:T(8,128)}, u32[]{:S(2)}) copy-start(f32[512,3,256]{0,2,1:T(8,128)} %copy.125) | copy-start | bytes 4718596
  1108.6 85.3 %copy-start.18 = (f32[512,3,256]{0,2,1:T(8,128)S(1)}, f32[512,3,256]{0,2,1:T(8,128)}, u32[]{:S(2)}) copy-start(f32[512,3,256]{0,2,1:T(8,128)} %copy.121) | copy-start | bytes 4718596
  1202.4 66.2 %copy-start.13 = (f32[256,2048]{1,0:T(8,128)S(1)}, f32[256,2048]{1,0:T(8,128)}, u32[]{:S(2)}) copy-start(f32[256,2048]{1,0:T(8,128)} %get-tuple-element.94) | copy-start | bytes 6291460
  (41 other events, 154.6 us)
Sparse Core Ops, SparseCore 0:
  10.2 66.1 all-gather.9
  78.3 52.8 all-gather.7
  133.3 27.9 all-gather.11
  194.6 217.7 all-reduce.3
  414.4 103.5 all-gather.13
  520.0 56.2 all-gather.15
  587.6 124.8 all-reduce.5
  719.3 54.3 all-gather.17
  809.6 71.4 reduce-scatter.6
  888.5 54.2 all-gather.19
  945.1 100.1 reduce-scatter.14
  1047.4 55.9 reduce-scatter.16
  1105.7 26.9 reduce-scatter.12
  1134.9 58.8 reduce-scatter.10
  1197.2 71.3 reduce-scatter.8
where the time goes:
time: 1290 us; the launch traced here: 1280 us
  waiting for transfers between devices  856 us (66%)
  matrix products  171 us (13%)
  other arithmetic  105 us (8%)
  local copies, waits for them, and re-layouts  89.7 us (7%)
  blocking collectives  41.6 us (3%)
  between operations  15 us (1%)
    psum x1, waiting for transfers between devices, local(): attn_total = lax.psum(attn_part, 'mp')  212 us
    psum x1, waiting for transfers between devices, local(): lax.psum(ffn_part.astype(jnp.bfloat16), 'mp').astype(jnp.float32)  124 us
    all_gather x1, waiting for transfers between devices, local(): lax.all_gather(gateup_weight.astype(jnp.bfloat16), 'dp', axis=0, tiled=True)  69.6 us
    reduce_scatter x1, waiting for transfers between devices, local(): lax.psum_scatter(middle_part.astype(jnp.bfloat16), 'mp', scatter_dimensio...  67.7 us
    all_gather x1, waiting for transfers between devices, local(): lax.all_gather(qkv_weight.astype(jnp.bfloat16), 'dp', axis=0, tiled=True)  61.7 us
    reduce_scatter x1, waiting for transfers between devices, local(): lax.psum_scatter(input_part.astype(jnp.bfloat16), 'mp', scatter_dimension...  59.7 us
    reduce_scatter x1, waiting for transfers between devices, local(): lax.psum_scatter(qkv_grad.astype(jnp.bfloat16), 'dp', scatter_dimension=0...  57.5 us
    all_gather x1, waiting for transfers between devices, local(): input_all = lax.all_gather(block_input, 'mp', axis=0, tiled=True)  54.8 us
  transfers between devices with their start and end apart: 15, of which 13 were waited for; matrix products, arithmetic and copies ran while one was open for 22% of the time, Pallas kernels for 0%

commit v1 on v0

--- a/solution.py
+++ b/solution.py
@@ -145,7 +145,9 @@
     gate_up = jnp.einsum("td,dcf->tcf", middle_low, gateup_full, preferred_element_type=jnp.float32)
     hidden_low = (jax.nn.gelu(gate_up[:, 0]) * gate_up[:, 1] * live_units).astype(jnp.bfloat16)
     ffn_part = jnp.dot(hidden_low, down_full, preferred_element_type=jnp.float32)
-    ffn_total = lax.psum(ffn_part.astype(jnp.bfloat16), "mp").astype(jnp.float32)
+    ffn_total = jnp.sum(lax.all_gather(ffn_part.astype(jnp.bfloat16), "mp"), axis=0).astype(
+        jnp.float32
+    )
     ffn_own = lax.dynamic_slice_in_dim(ffn_total, row_start, own_rows, 0)
     hidden_two = deep_alpha * middle + ffn_own
     output_rows, normed_two, inv_two = norm_forward(hidden_two, norm_params[2], norm_params[3])

time: 1290 us -> 1480 us (1.15)
  waiting for transfers between devices: 856 us -> 1030 us
  other arithmetic: 105 us -> 130 us
    all_gather x0 -> x1, waiting for transfers between devices: none -> 301 us  [local(): lax.all_gather(ffn_part.astype(jnp.bfloat16), 'mp')]
    psum x1 -> x0, waiting for transfers between devices: 124 us -> none  [local(): lax.psum(ffn_part.astype(jnp.bfloat16), 'mp').astype(jnp.float32)]
    reduce_sum x0 -> x1, other arithmetic: none -> 25.9 us  [local(): jnp.sum(lax.all_gather(ffn_part.astype(jnp.bfloat16), 'mp'), axis=0)]
  transfers between devices with their start and end apart: 15 -> 15, of which waited for: 13 -> 13; matrix products, arithmetic and copies ran while one was open for 22% -> 18% of each run, Pallas kernels for 0% -> 0%
where the time goes in v1:
time: 1480 us; the launch traced here: 1470 us
  waiting for transfers between devices  1030 us (70%)
  matrix products  171 us (12%)
  other arithmetic  130 us (9%)
  local copies, waits for them, and re-layouts  79.1 us (5%)
  blocking collectives  41.5 us (3%)
  between operations  15 us (1%)
    all_gather x1, waiting for transfers between devices, local(): lax.all_gather(ffn_part.astype(jnp.bfloat16), 'mp')  301 us
    psum x1, waiting for transfers between devices, local(): attn_total = lax.psum(attn_part, 'mp')  212 us
    all_gather x1, waiting for transfers between devices, local(): lax.all_gather(gateup_weight.astype(jnp.bfloat16), 'dp', axis=0, tiled=True)  69.5 us
    reduce_scatter x1, waiting for transfers between devices, local(): lax.psum_scatter(middle_part.astype(jnp.bfloat16), 'mp', scatter_dimensio...  67.7 us
    all_gather x1, waiting for transfers between devices, local(): lax.all_gather(qkv_weight.astype(jnp.bfloat16), 'dp', axis=0, tiled=True)  61.7 us
    reduce_scatter x1, waiting for transfers between devices, local(): lax.psum_scatter(input_part.astype(jnp.bfloat16), 'mp', scatter_dimension...  59.7 us
    reduce_scatter x1, waiting for transfers between devices, local(): lax.psum_scatter(qkv_grad.astype(jnp.bfloat16), 'dp', scatter_dimension=0...  57.6 us
    all_gather x1, waiting for transfers between devices, local(): input_all = lax.all_gather(block_input, 'mp', axis=0, tiled=True)  54.8 us
  transfers between devices with their start and end apart: 15, of which 13 were waited for; matrix products, arithmetic and copies ran while one was open for 18% of the time, Pallas kernels for 0%

profile of v1, /device:TPU:0, one launch (start us, length us, event | category | flops | bytes accessed | tf_op | source)
XLA Modules:
  0.0 1471.0 jit_solution(1026437086258964539)
XLA Ops:
  14.7 61.7 %all-gather.12.cloned.1.call-done = bf16[2048,3,256]{2,0,1:T(8,128)(2,1)} async-done(((bf16[512,3,256]{2,0,1:T(8,128)(2,1)}), bf16[2048,3,256]{2,0,1:T(8,128)(2,1)}) %all-gather.12.cloned.1.call-update) | async-done | bytes 3145744 | tf_op jit(solution)/shard_map/all_gather | solution.py:101
  76.4 54.8 %all-gather.10.cloned.1.call-done = bf16[2048,2048]{1,0:T(8,128)(2,1)} async-done(((bf16[256,2048]{1,0:T(8,128)(2,1)}), bf16[2048,2048]{1,0:T(8,128)(2,1)}) %all-gather.10.cloned.1.call-update) | async-done | bytes 8388624 | tf_op jit(solution)/shard_map/all_gather | solution.py:106
  131.2 11.6 fusion.6
  190.5 211.6 %all-reduce.3.cloned.1.call-done = f32[2048,2048]{1,0:T(8,128)} async-done(((f32[2048,2048]{1,0:T(8,128)}), f32[2048,2048]{1,0:T(8,128)}) %all-reduce.3.cloned.1.call-update) | async-done | bytes 16777232 | tf_op jit(solution)/shard_map/psum | solution.py:138
  402.1 16.0 %fusion.81 = (f32[2048]{0:T(1024)S(1)}, f32[2048,2048]{1,0:T(8,128)}) fusion(f32[2048,2048]{1,0:T(8,128)} %all-reduce.3.cloned.1.call-done, bf16[2048,2048]{1,0:T(8,128)(2,1)} %all-gather.10.cloned.1.call-done), kind=kLoop, calls=%fused_computation.166 | loop fusion | flops 16775168 | bytes 41951232 | tf_op jit(solution)/shard_map/reduce_sum | solution.py:40
  425.8 12.3 multiply_add_fusion
  438.1 69.5 %all-gather.16.cloned.1.call-done = bf16[2048,2,684]{0,1,2:T(2,128)(2,1)} async-done(((bf16[512,2,684]{0,1,2:T(2,128)(2,1)}), bf16[2048,2,684]{0,1,2:T(2,128)(2,1)}) %all-gather.16.cloned.1.call-update) | async-done | bytes 5603344 | tf_op jit(solution)/shard_map/all_gather | solution.py:103
  507.7 22.2 %fusion.2 = f32[2048,2,684]{0,2,1:T(8,128)} fusion(bf16[2048,2,684]{0,1,2:T(2,128)(2,1)} %all-gather.16.cloned.1.call-done, f32[2048,2048]{1,0:T(8,128)} %multiply_add_fusion), kind=kOutput, calls=%fused_computation.7 | convolution fusion | flops 11479810048 | bytes 33587200 | tf_op jit(solution)/shard_map/td,dcf->tcf/dot_general | solution.py:145
  535.4 30.5 %all-gather.18.cloned.1.call-done = bf16[684,2048]{1,0:T(8,128)(2,1)} async-done(((bf16[684,512]{1,0:T(8,128)(2,1)}), bf16[684,2048]{1,0:T(8,128)(2,1)}) %all-gather.18.cloned.1.call-update) | async-done | bytes 2801680 | tf_op jit(solution)/shard_map/all_gather | solution.py:104
  565.9 11.1 convolution_convert_fusion
  577.7 300.9 %all-gather.24.cloned.1.call-done = bf16[16384,2048]{1,0:T(8,128)(2,1)} async-done(((bf16[2048,2048]{1,0:T(8,128)(2,1)}), bf16[16384,2048]{1,0:T(8,128)(2,1)}) %all-gather.24.cloned.1.call-update) | async-done | bytes 67108880 | tf_op jit(solution)/shard_map/all_gather | solution.py:148
  878.6 25.9 %reduce_sum.168 = bf16[2048,2048]{1,0:T(8,128)(2,1)} reduce(bf16[8,2048,2048]{2,1,0:T(8,128)(2,1)} %bitcast.10, bf16[]{:T(256)} %constant.49.clone.1), dimensions={0}, to_apply=%region_5.6 | reduce | flops 29360128 | bytes 75497472 | tf_op jit(solution)/shard_map/reduce_sum | solution.py:148
  911.3 54.4 %all-gather.20.cloned.1.call-done = bf16[2048,2048]{1,0:T(8,128)(2,1)} async-done(((bf16[256,2048]{1,0:T(8,128)(2,1)}), bf16[2048,2048]{1,0:T(8,128)(2,1)}) %all-gather.20.cloned.1.call-update) | async-done | bytes 8388624 | tf_op jit(solution)/shard_map/all_gather | solution.py:157
  965.6 15.5 %fusion.36 = (bf16[2048,1,684]{0,2,1:T(8,128)(2,1)S(1)}, bf16[2048,1,684]{0,2,1:T(8,128)(2,1)S(1)}) fusion(f32[2048,2,684]{0,2,1:T(8,128)} %fusion.2, f32[684]{0:T(1024)S(1)} %fusion.66, bf16[2048,2048]{1,0:T(8,128)(2,1)} %all-gather.20.cloned.1.call-done, bf16[684,2048]{1,0:T(8,128)(2,1)} %all-gather.18.cloned.1.call-done), kind=kOutput, calls=%fused_computation.56 | convolution fusion | flops 5772828672 | bytes 28002992 | tf_op jit(solution)/shard_map/td,fd->tf/dot_general | solution.py:165
  983.6 17.9 %bitcast_convert_fusion.1 = bf16[2048,2048]{1,0:T(8,128)(2,1)} fusion(bf16[2048,2,684]{0,1,2:T(2,128)(2,1)} %all-gather.16.cloned.1.call-done, bf16[2048,1,684]{0,2,1:T(8,128)(2,1)S(1)} %get-tuple-element.102, bf16[2048,1,684]{0,2,1:T(8,128)(2,1)S(1)} %get-tuple-element.101), kind=kOutput, calls=%fused_computation.1 | convolution fusion | flops 11482611712 | bytes 19595264 | tf_op jit(solution)/shard_map/tcf,dcf->td/dot_general | solution.py:172
  1005.5 67.7 %reduce-scatter.7.cloned.1.call-done = bf16[256,2048]{1,0:T(8,128)(2,1)} async-done(((bf16[2048,2048]{1,0:T(8,128)(2,1)}), bf16[256,2048]{1,0:T(8,128)(2,1)}) %reduce-scatter.7.cloned.1.call-update) | async-done | bytes 1048592 | tf_op jit(solution)/shard_map/reduce_scatter | solution.py:179
  1080.4 18.7 %fusion.19 = bf16[2048,2,684]{0,2,1:T(8,128)(2,1)} fusion(f32[2048,2048]{1,0:T(8,128)} %multiply_add_fusion, bf16[2048,1,684]{0,2,1:T(8,128)(2,1)} %copy-done.49, bf16[2048,1,684]{0,2,1:T(8,128)(2,1)} %copy-done.48), kind=kOutput, calls=%fused_computation.39 | convolution fusion | flops 11493818368 | bytes 27983872 | tf_op jit(solution)/shard_map/td,tcf->dcf/dot_general | solution.py:175
  1112.3 22.5 %all-gather.22.cloned.1.call-done = bf16[2048,2048]{1,0:T(8,128)(2,1)} async-done(((bf16[256,2048]{1,0:T(8,128)(2,1)}), bf16[2048,2048]{1,0:T(8,128)(2,1)}) %all-gather.22.cloned.1.call-update) | async-done | bytes 8388624 | tf_op jit(solution)/shard_map/all_gather | solution.py:186
  1185.3 12.0 fusion.31
  1219.8 41.5 %all-reduce = (f32[]{:T(128)}, f32[4,2048]{1,0:T(4,128)S(1)}) all-reduce(f32[]{:T(128)} %convert_reduce_fusion, f32[4,2048]{1,0:T(4,128)S(1)} %pad_maximum_fusion.11), channel_id=1, replica_groups=mesh['dp'=4,'mp'=8] {'dp','mp'}, use_global_device_ids=true, to_apply=%region_18.19 | all-reduce | flops 8193 | bytes 65544 | tf_op jit(solution)/shard_map/psum | solution.py:247
  1279.1 16.4 %reduce-scatter.17.cloned.1.call-done = bf16[684,512]{1,0:T(8,128)(2,1)} async-done(((bf16[684,2048]{1,0:T(8,128)(2,1)}), bf16[684,512]{1,0:T(8,128)(2,1)}) %reduce-scatter.17.cloned.1.call-update) | async-done | bytes 700432 | tf_op jit(solution)/shard_map/reduce_scatter | solution.py:242
  1300.5 24.2 %reduce-scatter.13.cloned.1.call-done = bf16[256,512]{1,0:T(8,128)(2,1)} async-done(((bf16[256,2048]{1,0:T(8,128)(2,1)}), bf16[256,512]{1,0:T(8,128)(2,1)}) %reduce-scatter.13.cloned.1.call-update) | async-done | bytes 262160 | tf_op jit(solution)/shard_map/reduce_scatter | solution.py:236
  1328.2 57.6 %reduce-scatter.11.cloned.1.call-done = bf16[512,3,256]{0,2,1:T(8,128)(2,1)} async-done(((bf16[2048,3,256]{0,2,1:T(8,128)(2,1)}), bf16[512,3,256]{0,2,1:T(8,128)(2,1)}) %reduce-scatter.11.cloned.1.call-update) | async-done | bytes 786448 | tf_op jit(solution)/shard_map/reduce_scatter | solution.py:233
  1400.9 59.7 %reduce-scatter.9.cloned.1.call-done = bf16[256,2048]{1,0:T(8,128)(2,1)} async-done(((bf16[2048,2048]{1,0:T(8,128)(2,1)}), bf16[256,2048]{1,0:T(8,128)(2,1)}) %reduce-scatter.9.cloned.1.call-update) | async-done | bytes 1048592 | tf_op jit(solution)/shard_map/reduce_scatter | solution.py:227
  (217 shorter events, 219.6 us)
Async XLA Ops:
  7.2 69.1 %all-gather.12.cloned.1.call-start = ((), (), s32[]{:S(2)}) async-start(), calls=%async_computation.7 | async-start | bytes 3932160 | tf_op jit(solution)/shard_map/all_gather | solution.py:101
  9.7 121.5 %all-gather.10.cloned.1.call-start = ((), (), s32[]{:S(2)}) async-start(), calls=%async_computation.6 | async-start | bytes 9437184 | tf_op jit(solution)/shard_map/all_gather | solution.py:106
  10.5 164.0 %all-gather.14.cloned.1.call-start = ((), (), s32[]{:S(2)}) async-start(), calls=%async_computation.8 | async-start | bytes 1310720 | tf_op jit(solution)/shard_map/all_gather | solution.py:102
  11.3 390.8 %all-reduce.3.cloned.1.call-start = ((), (), s32[]{:S(2)}) async-start(), calls=%async_computation.9 | async-start | bytes 33554432 | tf_op jit(solution)/shard_map/psum | solution.py:138
  13.2 150.0 %copy-start.26 = (f32[512,64]{1,0:T(8,128)}, f32[512,64]{1,0:T(8,128)S(1)}, u32[]{:S(2)}) copy-start(f32[512,64]{1,0:T(8,128)S(1)} %get-tuple-element.124) | copy-start | bytes 393220
  184.2 323.5 %all-gather.16.cloned.1.call-start = ((), (), s32[]{:S(2)}) async-start(), calls=%async_computation.10 | async-start | bytes 7004160 | tf_op jit(solution)/shard_map/all_gather | solution.py:103
  188.0 377.9 %all-gather.18.cloned.1.call-start = ((), (), s32[]{:S(2)}) async-start(), calls=%async_computation.11 | async-start | bytes 3522560 | tf_op jit(solution)/shard_map/all_gather | solution.py:104
  190.4 688.3 %all-gather.24.cloned.1.call-start = ((), (), s32[]{:S(2)}) async-start(), calls=%async_computation.20 | async-start | bytes 75497472 | tf_op jit(solution)/shard_map/all_gather | solution.py:148
  535.4 41.6 %copy-start.24 = (bf16[2048,684]{0,1:T(8,128)(2,1)}, bf16[2048,684]{0,1:T(8,128)(2,1)S(1)}, u32[]{:S(2)}) copy-start(bf16[2048,684]{0,1:T(8,128)(2,1)S(1)} %multiply_convert_fusion.2) | copy-start | bytes 8404996
  577.1 388.6 %all-gather.20.cloned.1.call-start = ((), (), s32[]{:S(2)}) async-start(), calls=%async_computation.12 | async-start | bytes 9437184 | tf_op jit(solution)/shard_map/all_gather | solution.py:157
  911.2 161.9 %reduce-scatter.7.cloned.1.call-start = ((), (), s32[]{:S(2)}) async-start(), calls=%async_computation.13 | async-start | bytes 9437184 | tf_op jit(solution)/shard_map/reduce_scatter | solution.py:179
  1001.5 133.3 %all-gather.22.cloned.1.call-start = ((), (), s32[]{:S(2)}) async-start(), calls=%async_computation.14 | async-start | bytes 9437184 | tf_op jit(solution)/shard_map/all_gather | solution.py:186
  1080.4 181.0 %reduce-scatter.15.cloned.1.call-start = ((), (), s32[]{:S(2)}) async-start(), calls=%async_computation.18 | async-start | bytes 7045120 | tf_op jit(solution)/shard_map/reduce_scatter | solution.py:239
  1099.1 196.3 %reduce-scatter.17.cloned.1.call-start = ((), (), s32[]{:S(2)}) async-start(), calls=%async_computation.19 | async-start | bytes 3522560 | tf_op jit(solution)/shard_map/reduce_scatter | solution.py:242
  1111.5 23.2 %copy-start.30 = (bf16[256,2048]{1,0:T(8,128)(2,1)S(1)}, bf16[256,2048]{1,0:T(8,128)(2,1)}, u32[]{:S(2)}) copy-start(bf16[256,2048]{1,0:T(8,128)(2,1)} %all-gather.14.cloned.1.call-done) | copy-start | bytes 3145732
  1111.5 213.2 %reduce-scatter.13.cloned.1.call-start = ((), (), s32[]{:S(2)}) async-start(), calls=%async_computation.17 | async-start | bytes 1310720 | tf_op jit(solution)/shard_map/reduce_scatter | solution.py:236
  1183.1 202.7 %reduce-scatter.11.cloned.1.call-start = ((), (), s32[]{:S(2)}) async-start(), calls=%async_computation.16 | async-start | bytes 3932160 | tf_op jit(solution)/shard_map/reduce_scatter | solution.py:233
  1197.3 263.3 %reduce-scatter.9.cloned.1.call-start = ((), (), s32[]{:S(2)}) async-start(), calls=%async_computation.15 | async-start | bytes 9437184 | tf_op jit(solution)/shard_map/reduce_scatter | solution.py:227
  1213.0 48.4 %copy-start.4 = (f32[512,2,684]{0,1,2:T(2,128)S(1)}, f32[512,2,684]{0,1,2:T(2,128)}, u32[]{:S(2)}) copy-start(f32[512,2,684]{0,1,2:T(2,128)} %param.27) | copy-start | bytes 8404996
  1274.0 21.4 %copy-start.19 = (f32[684,512]{1,0:T(8,128)S(1)}, f32[684,512]{1,0:T(8,128)}, u32[]{:S(2)}) copy-start(f32[684,512]{1,0:T(8,128)} %param.28) | copy-start | bytes 4202500
  1274.0 21.4 %copy-start.29 = (f32[684,512]{1,0:T(8,128)S(1)}, f32[684,512]{1,0:T(8,128)}, u32[]{:S(2)}) copy-start(f32[684,512]{1,0:T(8,128)} %param.33) | copy-start | bytes 4202500
  1300.5 85.3 %copy-start.17 = (f32[512,3,256]{0,2,1:T(8,128)S(1)}, f32[512,3,256]{0,2,1:T(8,128)}, u32[]{:S(2)}) copy-start(f32[512,3,256]{0,2,1:T(8,128)} %copy.125) | copy-start | bytes 4718596
  1300.5 85.3 %copy-start.18 = (f32[512,3,256]{0,2,1:T(8,128)S(1)}, f32[512,3,256]{0,2,1:T(8,128)}, u32[]{:S(2)}) copy-start(f32[512,3,256]{0,2,1:T(8,128)} %copy.121) | copy-start | bytes 4718596
  1394.3 66.3 %copy-start.13 = (f32[256,2048]{1,0:T(8,128)S(1)}, f32[256,2048]{1,0:T(8,128)}, u32[]{:S(2)}) copy-start(f32[256,2048]{1,0:T(8,128)} %get-tuple-element.94) | copy-start | bytes 6291460
  (41 other events, 135.9 us)
Sparse Core Ops, SparseCore 0:
  10.2 66.1 all-gather.11
  78.3 52.8 all-gather.9
  133.3 27.9 all-gather.13
  184.3 217.7 all-reduce.2
  404.1 103.5 all-gather.15
  509.7 56.2 all-gather.17
  577.2 301.3 all-gather.23
  911.4 54.2 all-gather.19
  1001.6 71.5 reduce-scatter.6
  1080.5 54.2 all-gather.21
  1137.1 100.1 reduce-scatter.14
  1239.4 55.9 reduce-scatter.16
  1297.7 26.9 reduce-scatter.12
  1326.9 58.9 reduce-scatter.10
  1389.1 71.3 reduce-scatter.8
